TPU v7x, 512 devices: a whole 4x8x8 slice. The times are simulated.
512 devices in a mesh: seq: 64 (over y, z), head: 8 (over x, core).
Axes of the slice: x: 4, y: 8, z: 8, core: 2. Of those that a mesh axis runs over, the one named last changes fastest.
Arguments:
- query_input: bfloat16 [16384, 2048], P('seq', 'head'), may hold values from -6 to 6
- key_input: bfloat16 [16384, 2048], P('seq', 'head'), may hold values from -6 to 6
- value_input: bfloat16 [16384, 4096], P('seq', 'head'), may hold values from -6 to 6
- kernel_taps: float32 [2, 4, 2048], P(None, None, 'head'), may hold values from -3 to 3
- input_gate: float32 [8, 16384], P('head', 'seq'), may hold values from -6 to 300
- forget_gate: float32 [8, 16384], P('head', 'seq'), may hold values from -0.5 to 16
- request_lengths: int32 [4], replicated, may hold values from 1 to 8192, as said below
- output_weight: bfloat16 [4096, 2048], P('head'), may hold values from -0.09375 to 0.09375
Outputs:
- mixed_out: bfloat16 [16384, 2048], P('seq', 'head')
Inputs may be any that keep to these rules, and one draw needn't show every extreme that they name: `request_lengths`: the lengths sum to 16384; the longest request has exactly 8192 tokens.
All inputs are finite; a program needn't handle non-finite values.
Results may differ from a plain program's by a relative error of at most 0.012.
Values may be sent and summed in bfloat16 or wider, within the bound.
A program may use at most 128 MiB of HBM per device.

v0:
```python
import math

import jax
import jax.numpy as jnp
from jax import lax
from jax.sharding import PartitionSpec as P

very_negative = -1e30


def entering(part, axis, combine, identity):
    place = lax.axis_index(axis)
    gathered = jax.tree.map(lambda a: lax.all_gather(a, axis), part)
    state = jax.tree.map(lambda a, e: jnp.zeros_like(a) + jnp.asarray(e, a.dtype), part, identity)

    def one(turn, state):
        return combine(
            state, jax.tree.map(lambda a: lax.dynamic_index_in_dim(a, turn, 0, False), gathered)
        )

    return lax.fori_loop(0, place, one, state)


def shifted_2(value, axis, steps):
    count = lax.axis_size(axis)
    initial, last = (max(0, -steps), min(count, count - steps))
    return lax.ppermute(value, axis, [(source, source + steps) for source in range(initial, last)])


def conv_silu(extended, wide_segment, kernel_part, segments):
    length = segments.shape[0]
    taps = kernel_part.shape[0]
    running = jnp.zeros((length, extended.shape[1]), jnp.float32)
    for shift_by in range(taps):
        piece_rows = extended[taps - 1 - shift_by : taps - 1 - shift_by + length].astype(
            jnp.float32
        )
        same_req = (wide_segment[taps - 1 - shift_by : taps - 1 - shift_by + length] == segments)[
            :, None
        ]
        running = running + jnp.where(same_req, kernel_part[shift_by][None, :] * piece_rows, 0.0)
    return jax.nn.silu(running).astype(jnp.bfloat16)


def block_pass(state, block):
    memory, normal, stabilizer, segment_prev = state
    query_block, key_block, value_block, forget_block, input_block, segment_block = block
    block_len = query_block.shape[0]
    key_scale = 1.0 / math.sqrt(query_block.shape[2])
    cumulative = jnp.cumsum(forget_block, axis=1)
    positions = jnp.arange(block_len, dtype=jnp.int32)
    allowed = (positions[None, :] <= positions[:, None]) & (
        segment_block[None, :] == segment_block[:, None]
    )
    log_weight = jnp.where(
        allowed[None],
        input_block[:, None, :] + cumulative[:, :, None] - cumulative[:, None, :],
        very_negative,
    )
    linked = segment_block == segment_prev
    carried = jnp.where(linked[None, :], stabilizer[:, None] + cumulative, very_negative)
    row_max = jnp.maximum(jnp.max(log_weight, axis=2), carried)
    scores = (
        jnp.einsum("thd,shd->hts", query_block, key_block, preferred_element_type=jnp.float32)
        * key_scale
    )
    weights = scores * jnp.exp(log_weight - row_max[:, :, None])
    reach_share = jnp.exp(carried - row_max)
    scaled_query = query_block.astype(jnp.float32) * key_scale
    from_memory = jnp.einsum("thd,hdv->thv", scaled_query, memory, precision=lax.Precision.HIGHEST)
    from_normal = jnp.einsum("thd,hd->ht", scaled_query, normal, precision=lax.Precision.HIGHEST)
    numerator = jnp.einsum(
        "hts,shv->thv",
        weights.astype(jnp.bfloat16),
        value_block,
        preferred_element_type=jnp.float32,
    )
    numerator = numerator + reach_share.T[:, :, None] * from_memory
    denominator = jnp.sum(weights, axis=2) + reach_share * from_normal
    segment_last = segment_block[block_len - 1]
    tail_weight = jnp.where(
        (segment_block == segment_last)[None, :],
        input_block + cumulative[:, -1:] - cumulative,
        very_negative,
    )
    tail_carry = jnp.where(
        segment_prev == segment_last, stabilizer + cumulative[:, -1], very_negative
    )
    stabilizer_new = jnp.maximum(jnp.max(tail_weight, axis=1), tail_carry)
    factor = jnp.exp(tail_weight - stabilizer_new[:, None])
    weighted_keys = key_block.astype(jnp.float32) * factor.T[:, :, None]
    decay_share = jnp.exp(tail_carry - stabilizer_new)
    memory_new = decay_share[:, None, None] * memory + jnp.einsum(
        "shd,shv->hdv",
        weighted_keys.astype(jnp.bfloat16),
        value_block,
        preferred_element_type=jnp.float32,
    )
    normal_new = decay_share[:, None] * normal + jnp.sum(weighted_keys, axis=0)
    return (
        (memory_new, normal_new, stabilizer_new, segment_last),
        (numerator, denominator, row_max),
    )


def combine_states(before_part, after_part):
    memory_one, normal_one, stab_one, decay_one = before_part
    memory_two, normal_two, stab_two, decay_two = after_part
    shifted = stab_one + decay_two
    stab_both = jnp.maximum(shifted, stab_two)
    share_one = jnp.exp(shifted - stab_both)
    share_two = jnp.exp(stab_two - stab_both)
    memory_both = share_one[:, None, None] * memory_one + share_two[:, None, None] * memory_two
    normal_both = share_one[:, None] * normal_one + share_two[:, None] * normal_two
    return (memory_both, normal_both, stab_both, decay_one + decay_two)


def incoming_state(memory_part, normal_part, stab_part, through_part):
    identity_state = (
        jnp.zeros_like(memory_part),
        jnp.zeros_like(normal_part),
        jnp.full(stab_part.shape, very_negative, jnp.float32),
        jnp.zeros_like(through_part),
    )
    return entering(
        (memory_part, normal_part, stab_part, through_part), "seq", combine_states, identity_state
    )


def unstack_rows(outputs, tok_rows):
    numerator, denominator, row_max = outputs
    heads_here = numerator.shape[2]
    numerator = numerator.reshape(tok_rows, heads_here, numerator.shape[3])
    denominator = denominator.transpose(1, 0, 2).reshape(heads_here, tok_rows)
    row_max = row_max.transpose(1, 0, 2).reshape(heads_here, tok_rows)
    return (numerator, denominator, row_max)


def on_device(
    query_input,
    key_input,
    value_input,
    kernel_taps,
    input_gate,
    forget_gate,
    request_lengths,
    output_weight,
):
    tok_rows = query_input.shape[0]
    heads_here = input_gate.shape[0]
    key_width = query_input.shape[1] // heads_here
    value_width = value_input.shape[1] // heads_here
    kernel_len = kernel_taps.shape[1]
    offset = lax.axis_index("seq") * tok_rows
    starts = jnp.cumsum(request_lengths) - request_lengths

    def segment_of(position):
        return jnp.sum((starts[None, :] <= position[:, None]).astype(jnp.int32), axis=1) - 1

    segments = segment_of(offset + jnp.arange(tok_rows, dtype=jnp.int32))
    wide_segment = segment_of(
        offset - (kernel_len - 1) + jnp.arange(tok_rows + kernel_len - 1, dtype=jnp.int32)
    )
    segment_before = segment_of(jnp.reshape(offset - 1, (1,)))[0]
    tail_query, tail_key = shifted_2(
        (query_input[tok_rows - (kernel_len - 1) :], key_input[tok_rows - (kernel_len - 1) :]),
        "seq",
        1,
    )
    query_conv = conv_silu(
        jnp.concatenate([tail_query, query_input]), wide_segment, kernel_taps[0], segments
    )
    key_conv = conv_silu(
        jnp.concatenate([tail_key, key_input]), wide_segment, kernel_taps[1], segments
    )
    query_heads = query_conv.reshape(tok_rows, heads_here, key_width)
    key_heads = key_conv.reshape(tok_rows, heads_here, key_width)
    value_heads = value_input.reshape(tok_rows, heads_here, value_width)
    log_forget = jax.nn.log_sigmoid(forget_gate)
    cumulative = jnp.cumsum(log_forget, axis=1)
    block_len = min(512, tok_rows)
    block_count = tok_rows // block_len
    blocks = (
        query_heads.reshape(block_count, block_len, heads_here, key_width),
        key_heads.reshape(block_count, block_len, heads_here, key_width),
        value_heads.reshape(block_count, block_len, heads_here, value_width),
        log_forget.reshape(heads_here, block_count, block_len).transpose(1, 0, 2),
        input_gate.reshape(heads_here, block_count, block_len).transpose(1, 0, 2),
        segments.reshape(block_count, block_len),
    )
    segment_last = segments[tok_rows - 1]
    through = jnp.where(segment_before == segment_last, cumulative[:, -1], very_negative)
    tail_weight = jnp.where(
        (segments == segment_last)[None, :],
        input_gate + cumulative[:, -1:] - cumulative,
        very_negative,
    )
    stab_local = jnp.max(tail_weight, axis=1)
    factor = jnp.exp(tail_weight - stab_local[:, None])
    weighted_keys = key_heads.astype(jnp.float32) * factor.T[:, :, None]
    memory_local = jnp.einsum(
        "shd,shv->hdv",
        weighted_keys.astype(jnp.bfloat16),
        value_heads,
        preferred_element_type=jnp.float32,
    )
    normal_local = jnp.sum(weighted_keys, axis=0)
    memory_in, normal_in, stab_in, _ = incoming_state(
        memory_local, normal_local, stab_local, through
    )
    _, outputs = lax.scan(block_pass, (memory_in, normal_in, stab_in, segment_before), blocks)
    numerator, denominator, row_max = unstack_rows(outputs, tok_rows)
    floor_value = jnp.maximum(jnp.abs(denominator), 1.0).T
    head_out = (
        (numerator / floor_value[:, :, None])
        .reshape(tok_rows, heads_here * value_width)
        .astype(jnp.bfloat16)
    )
    partial_value = jnp.dot(head_out, output_weight, preferred_element_type=jnp.float32)
    mixed_out = lax.psum_scatter(partial_value, "head", scatter_dimension=1, tiled=True)
    return mixed_out.astype(jnp.bfloat16)


def solution(mesh):
    placed = (
        P("seq", "head"),
        P("seq", "head"),
        P("seq", "head"),
        P(None, None, "head"),
        P("head", "seq"),
        P("head", "seq"),
        P(),
        P("head", None),
    )
    return jax.shard_map(
        on_device, mesh=mesh, in_specs=placed, out_specs=P("seq", "head"), check_vma=False
    )
```

profile of v0, /device:TPU:8, one launch (start us, length us, event | category | flops | bytes accessed | tf_op | source)
XLA Modules:
  0.0 547.8 jit_solution(15959032579842037206)
XLA Ops:
  6.5 0.0 copy-start
  6.5 0.9 slice.116
  7.4 0.1 copy.37
  7.6 4.3 collective-permute-start.1
  11.9 0.8 reduce-window.21
  12.7 1.3 fusion.24
  14.1 0.1 convert_reduce_fusion.1
  14.1 0.7 slice.124
  14.8 0.1 convert_reduce_fusion
  14.9 0.7 fusion.22
  15.6 0.3 reduce-window.22
  15.9 0.2 slice_reduce_fusion
  16.1 0.2 reduce-window.23
  16.3 0.1 broadcast.282
  16.4 0.6 slice.134
  17.0 0.9 fusion.30
  17.8 0.8 slice_compare_fusion.3
  18.6 1.9 fusion.29
  20.5 0.6 subtract_exponential_fusion.1
  21.1 1.0 copy.36
  22.2 0.0 collective-permute-done.1
  22.2 0.5 fusion.8
  22.6 2.0 fusion.16
  24.6 0.0 all-gather.6.cloned.1.call-update
  24.7 0.0 reduce-scatter.2.cloned.1.call-start
  24.7 0.1 copy.34
  24.9 4.3 collective-permute-start
  29.2 0.1 copy.33
  30.6 1.3 dynamic-slice.3
  31.9 1.4 dynamic-update-slice.1
  33.3 1.4 fusion.25
  34.7 133.9 %all-reduce.2 = (f32[64]{0:T(128)S(1)}, f32[64]{0:T(128)S(1)}) all-reduce(f32[64]{0:T(128)S(1)} %fusion.25, f32[64]{0:T(128)S(1)} %dynamic-update-slice.1), channel_id=2, replica_groups=mesh['seq'=64,'head'=8] {'seq'}, use_global_device_ids=true, to_apply=%add | all-reduce | flops 128 | bytes 1024
  168.6 0.1 bitcast_add_fusion.2
  168.7 0.2 select_reduce_fusion
  168.9 59.5 %all-gather.3 = f32[64,1,256]{2,1,0:T(1,128)S(1)} all-gather(f32[1,1,256]{2,1,0:T(1,128)S(1)} %bitcast.101), channel_id=4, replica_groups=mesh['seq'=64,'head'=8] {'seq'}, dimensions={0}, use_global_device_ids=true | all-gather | bytes 66560 | tf_op jit(solution)/shard_map/all_gather | solution.py:13
  228.3 0.0 collective-permute-done
  228.3 0.4 multiply_convert_fusion.1
  228.7 23.4 %all-gather.6.cloned.1.call-done = f32[16384,512]{1,0:T(8,128)} async-done(((f32[256,512]{1,0:T(8,128)}), f32[16384,512]{1,0:T(8,128)}) %all-gather.6.cloned.1.call-update) | async-done | bytes 33554448 | tf_op jit(solution)/shard_map/all_gather | solution.py:13
  252.2 0.0 copy-start.1
  252.2 31.8 %while.3 = (s32[]{:T(128)}, f32[1,256,512]{2,1,0:T(8,128)S(1)}, f32[1,256]{1,0:T(1,128)S(1)}, f32[1]{0:T(128)}, s32[]{:T(128)}, /*index=5*/f32[64,1]{0,1:T(1,128...) while((s32[]{:T(128)}, f32[1,256,512]{2,1,0:T(8,128)S(1)}, ...), condition=%wide.region_10.11_spmd, body=%wide.region_9.10_spmd.sunk | while | flops 393993 | bytes 1576195 | solution.py:21
  252.2 0.7 constant_dynamic-slice_fusion.3
  254.9 1.3 bitcast_add_fusion.5
  256.2 0.7 constant_dynamic-slice_fusion.3
  258.8 1.3 bitcast_add_fusion.5
  260.2 0.7 constant_dynamic-slice_fusion.3
  262.8 1.3 bitcast_add_fusion.5
  264.1 0.7 constant_dynamic-slice_fusion.3
  266.8 1.3 bitcast_add_fusion.5
  268.1 0.7 constant_dynamic-slice_fusion.3
  270.8 1.3 bitcast_add_fusion.5
  272.1 0.7 constant_dynamic-slice_fusion.3
  274.7 1.3 bitcast_add_fusion.5
  276.1 0.7 constant_dynamic-slice_fusion.3
  278.7 1.3 bitcast_add_fusion.5
  280.0 0.7 constant_dynamic-slice_fusion.3
  282.7 1.3 bitcast_add_fusion.5
  284.0 0.2 fusion.7
  284.3 0.3 fusion.31
  284.5 0.2 convolution_bitcast_fusion.1
  284.8 0.7 fusion.4
  285.5 2.1 fusion.32
  287.6 0.0 reduce-scatter.2.cloned.1.call-update
  287.6 251.7 %reduce-scatter.2.cloned.1.call-done = f32[256,256]{1,0:T(8,128)} async-done(((f32[256,2048]{1,0:T(8,128)}), f32[256,256]{1,0:T(8,128)}) %reduce-scatter.2.cloned.1.call-update) | async-done | bytes 262160 | tf_op jit(solution)/shard_map/reduce_scatter | solution.py:220
  539.3 1.6 convert_element_type.94
  (28 shorter events, 0.3 us)
Async XLA Ops:
  6.5 279.0 %copy-start = (bf16[512,2048]{1,0:T(8,128)(2,1)S(1)}, bf16[512,2048]{1,0:T(8,128)(2,1)}, u32[]{:S(2)}) copy-start(bf16[512,2048]{1,0:T(8,128)(2,1)} %param.17) | copy-start | bytes 6291460
  6.5 162.1 %copy-start.3 = (f32[1,256]{1,0:T(1,128)S(1)}, f32[1,256]{1,0:T(1,128)}, u32[]{:S(2)}) copy-start(f32[1,256]{1,0:T(1,128)} %param.14) | copy-start | bytes 3076
  6.5 18.2 %copy-start.2 = (bf16[256,256]{1,0:T(8,128)(2,1)S(1)}, bf16[256,256]{1,0:T(8,128)(2,1)}, u32[]{:S(2)}) copy-start(bf16[256,256]{1,0:T(8,128)(2,1)} %param.10) | copy-start | bytes 393220
  6.5 245.6 %all-gather.6.cloned.1.call-start = ((), (), s32[]{:S(2)}) async-start(), calls=%async_computation.2 | async-start | bytes 34078720 | tf_op jit(solution)/shard_map/all_gather | solution.py:13
  7.6 14.6 %collective-permute-start.1 = (bf16[3,256]{0,1:T(8,128)(2,1)S(1)}, bf16[3,256]{0,1:T(8,128)(2,1)S(1)}, u32[]{:S(2)}, u32[]{:S(2)}) collective-permute-start(bf16[3,256]{0,1:T(8,128)(2,1)S(1)} %copy.37), channel_id=1, source_target_pairs={{0,8},{8,16},{16,24},{24,32},{32,40},{40,48},{48,56},{56,64},{64,7... | collective-permute-start | bytes 4616 | tf_op jit(solution)/shard_map/ppermute | solution.py:27
  24.7 514.6 %reduce-scatter.2.cloned.1.call-start = ((), (), s32[]{:S(2)}) async-start(), calls=%async_computation.1 | async-start | bytes 2359296 | tf_op jit(solution)/shard_map/reduce_scatter | solution.py:220
  24.9 203.5 %collective-permute-start = (bf16[3,256]{0,1:T(8,128)(2,1)S(1)}, bf16[3,256]{0,1:T(8,128)(2,1)S(1)}, u32[]{:S(2)}, u32[]{:S(2)}) collective-permute-start(bf16[3,256]{0,1:T(8,128)(2,1)S(1)} %copy.34), channel_id=1, source_target_pairs={{0,8},{8,16},{16,24},{24,32},{32,40},{40,48},{48,56},{56,64},{64,7... | collective-permute-start | bytes 4616 | tf_op jit(solution)/shard_map/ppermute | solution.py:27
  252.2 32.4 %copy-start.1 = (bf16[256,512]{1,0:T(8,128)(2,1)S(1)}, bf16[256,512]{1,0:T(8,128)(2,1)}, u32[]{:S(2)}) copy-start(bf16[256,512]{1,0:T(8,128)(2,1)} %param.12) | copy-start | bytes 786436
Sparse Core Ops, SparseCore 0:
  24.8 227.2 all-gather.5
  287.7 251.5 reduce-scatter.1
where the time goes:
time: 553 us; the launch traced here: 548 us
  waiting for transfers between devices  275 us (50%)
  blocking collectives  193 us (35%)
  other arithmetic  21.4 us (4%)
  loops' own time  16.2 us (3%)
  between operations  14.9 us (3%)
  local copies, waits for them, and re-layouts  12.7 us (2%)
  starting transfers between devices  8.59 us (2%)
    reduce_scatter x1, waiting for transfers between devices, on_device(): lax.psum_scatter(partial_value, 'head', scatter_dimension=1, tiled=True)  252 us
    unnamed x1, blocking collectives  134 us
    all_gather x1, blocking collectives, entering(): gathered = jax.tree.map(lambda a: lax.all_gather(a, axis), part)  59.5 us
    all_gather x1, waiting for transfers between devices, entering(): gathered = jax.tree.map(lambda a: lax.all_gather(a, axis), part)  23.4 us
    another operation x1, loops' own time, entering(): return lax.fori_loop(0, place, one, state)  16.2 us
  transfers between devices with their start and end apart: 4, of which 2 were waited for; matrix products, arithmetic and copies ran while one was open for 3% of the time, Pallas kernels for 0%

commit v1 on v0

v1 whole, which is shorter than its diff:
```python
import functools

import jax
import jax.numpy as jnp
from jax import lax
from jax.experimental import pallas as pl
from jax.experimental.pallas import tpu as pltpu
from jax.sharding import PartitionSpec as P

MESH = pl.DeviceIdType.MESH
NEG = -1e30
SIDE = 8
F32 = jnp.float32
BF16 = jnp.bfloat16


def kernel(
    shards,
    chips,
    len_ref,
    q_ref,
    k_ref,
    v_ref,
    taps_ref,
    ig_ref,
    fg_ref,
    wo_hbm,
    out_ref,
    wo_ref,
    ext_ref,
    halo_send,
    halo_recv,
    scal_ref,
    stab_rows,
    thr_rows,
    m_rows,
    a_rows,
    b_rows,
    own_tiles,
    got_tiles,
    back_tiles,
    mem_tiles,
    norm_z,
    norm_y,
    num_ref,
    pair_send,
    pair_recv,
    x_send,
    x_recv,
    wo_sem,
    halo_sem,
    scal_sem,
    norm_sem,
    tile_sem,
    pair_ssem,
    pair_rsem,
    x_ssem,
    x_rsem,
):
    tokens, width = q_ref.shape
    values = v_ref.shape[1]
    scale = 1.0 / (width**0.5)
    me = lax.axis_index("seq")
    head = lax.axis_index("head")
    my_y, my_z = me // SIDE, me % SIDE
    my_x, my_c = head // 2, head % 2
    rows = shards // SIDE

    def seq_at(index):
        return {"seq": index}

    def head_at(index):
        return {"head": index}

    def remote(src, dst, ssem, rsem, where):
        return pltpu.make_async_remote_copy(
            src_ref=src, dst_ref=dst, send_sem=ssem, recv_sem=rsem, device_id=where, device_id_type=MESH
        )

    wo_copy = pltpu.make_async_copy(wo_hbm, wo_ref, wo_sem)
    wo_copy.start()

    barrier = pltpu.get_barrier_semaphore()

    def greet(step, carry):
        pl.semaphore_signal(
            barrier, inc=1, device_id=seq_at((me + step) % shards), device_id_type=MESH
        )
        return carry

    lax.fori_loop(1, shards, greet, 0)
    partner = 2 * my_x + (1 - my_c)
    pl.semaphore_signal(barrier, inc=1, device_id=head_at(partner), device_id_type=MESH)
    for step in range(1, chips):
        pl.semaphore_signal(
            barrier,
            inc=1,
            device_id=head_at(2 * ((my_x + step) % chips) + my_c),
            device_id_type=MESH,
        )

    offset = me * tokens
    starts = [jnp.int32(0)]
    for r in range(len_ref.shape[0] - 1):
        starts.append(starts[-1] + len_ref[r])

    def request_start(position):
        found = jnp.zeros_like(position)
        for start in starts[1:]:
            found = jnp.where(start <= position, start, found)
        return found

    t_col = lax.broadcasted_iota(jnp.int32, (tokens, 128), 0)
    begin_col = request_start(t_col + offset) - offset
    s_row = lax.broadcasted_iota(jnp.int32, (1, tokens), 1)
    last_begin = jnp.int32(0)
    for start in starts[1:]:
        last_begin = jnp.where(start <= offset + (tokens - 1), start, last_begin)
    last_begin = last_begin - offset

    fg = fg_ref[...]
    ig = ig_ref[...]
    log_forget = -(jnp.maximum(-fg, 0.0) + jnp.log1p(jnp.exp(-jnp.abs(fg))))
    hi = log_forget.astype(BF16)
    rest = log_forget - hi.astype(F32)
    mid = rest.astype(BF16)
    low = (rest - mid.astype(F32)).astype(BF16)
    pieces = jnp.concatenate(
        [hi.astype(F32), mid.astype(F32), low.astype(F32), jnp.zeros((5, tokens), F32)], axis=0
    ).astype(BF16)
    t_full = lax.broadcasted_iota(jnp.int32, (tokens, tokens), 0)
    s_full = lax.broadcasted_iota(jnp.int32, (tokens, tokens), 1)
    upper = jnp.where(t_full <= s_full, 1.0, 0.0).astype(BF16)
    cum_row = jnp.sum(
        jnp.dot(pieces, upper, preferred_element_type=F32), axis=0, keepdims=True
    )
    cum_last = cum_row[:, tokens - 1 : tokens]
    gain_row = ig - cum_row
    tail_row = jnp.where(s_row >= last_begin, gain_row + cum_last, NEG)
    stab = jnp.max(tail_row, axis=1, keepdims=True)
    factor_row = jnp.exp(tail_row - stab)
    through = jnp.where(last_begin < 0, cum_last, NEG)
    scal_ref[me] = jnp.concatenate(
        [jnp.broadcast_to(stab, (1, 128)), jnp.broadcast_to(through, (1, 128))], axis=0
    )
    turned = jnp.transpose(
        jnp.concatenate([cum_row, factor_row, jnp.zeros((126, tokens), F32)], axis=0)
    )
    cum_col = turned[:, 0:1]
    factor_col = turned[:, 1:2]

    halo_send[0] = k_ref[tokens - 16 : tokens, :]
    halo_send[1] = q_ref[tokens - 16 : tokens, :]

    pl.semaphore_wait(barrier, shards - 1 + chips)

    halo = remote(
        halo_send, halo_recv, halo_sem.at[0], halo_sem.at[1], seq_at((me + 1) % shards)
    )
    halo.start()

    def z_peer(step):
        return my_y * SIDE + (my_z + step) % SIDE

    def y_peer(step):
        return ((my_y + step) % rows) * SIDE + my_z

    for step in range(1, SIDE):
        remote(
            scal_ref.at[me], scal_ref.at[me], scal_sem.at[0], scal_sem.at[1], seq_at(z_peer(step))
        ).start()

    def conv_silu(source, which, tail):
        ext_ref[0:8, :] = halo_recv[tail, 8:16, :].astype(F32)
        ext_ref[8 : 8 + tokens, :] = source[...].astype(F32)
        running = taps_ref[which, 0:1, :] * ext_ref[8 : 8 + tokens, :]
        for lag in range(1, taps_ref.shape[1]):
            keep = (t_col - lag) >= begin_col
            keep = jnp.concatenate([keep.astype(F32)] * (width // 128), axis=1) > 0.0
            shifted = ext_ref[8 - lag : 8 - lag + tokens, :]
            running = running + jnp.where(keep, taps_ref[which, lag : lag + 1, :] * shifted, 0.0)
        return (running / (1.0 + jnp.exp(-running))).astype(BF16)

    halo.wait_recv()
    key = conv_silu(k_ref, 1, 0)
    weighted = key.astype(F32) * factor_col
    value = v_ref[...]
    memory = lax.dot_general(
        weighted.astype(BF16), value, (((0,), (0,)), ((), ())), preferred_element_type=F32
    ).astype(BF16)
    tile_rows = width // 16
    for c in range(values // 128):
        own_tiles[c * tile_rows : (c + 1) * tile_rows] = memory[
            :, c * 128 : (c + 1) * 128
        ].reshape(tile_rows, 16, 128)
    normal = jnp.sum(weighted, axis=0, keepdims=True)
    norm_z[my_z] = jnp.concatenate([normal[:, 0:128], normal[:, 128:256]], axis=0)

    def send_tile(step, carry):
        peer = (me + step) % shards
        remote(
            own_tiles.at[peer], got_tiles.at[me], tile_sem.at[0], tile_sem.at[1], seq_at(peer)
        ).start()
        return carry

    some = pl.ds(0, SIDE - 1)
    remote(
        scal_ref.at[some], scal_ref.at[some], scal_sem.at[0], scal_sem.at[1], seq_at(me)
    ).wait_recv()
    mine = pl.ds(my_y * SIDE, SIDE)
    for step in range(1, rows):
        remote(
            scal_ref.at[mine],
            scal_ref.at[mine],
            scal_sem.at[2],
            scal_sem.at[3],
            seq_at(y_peer(step)),
        ).start()
    lax.fori_loop(1, shards, send_tile, 0)
    for step in range(1, SIDE):
        remote(
            norm_z.at[my_z], norm_z.at[my_z], norm_sem.at[0], norm_sem.at[1], seq_at(z_peer(step))
        ).start()
    got_tiles[me] = own_tiles[me]

    query = conv_silu(q_ref, 0, 1)
    scores = (
        lax.dot_general(query, key, (((1,), (1,)), ((), ())), preferred_element_type=F32) * scale
    )

    most = pl.ds(0, (rows - 1) * SIDE)
    remote(
        scal_ref.at[most], scal_ref.at[most], scal_sem.at[2], scal_sem.at[3], seq_at(me)
    ).wait_recv()
    level = jnp.full((1, 128), NEG, F32)
    for s in range(shards):
        pair = scal_ref[s]
        stab_s, thr_s = pair[0:1, :], pair[1:2, :]
        m_rows[s : s + 1, :] = level
        carried_on = level + thr_s
        level = jnp.maximum(stab_s, carried_on)
        stab_rows[s : s + 1, :] = stab_s - level
        thr_rows[s : s + 1, :] = carried_on - level
    a_rows[...] = jnp.exp(thr_rows[...])
    b_rows[...] = jnp.exp(stab_rows[...])

    some_norm = pl.ds(0, SIDE - 1)
    remote(
        norm_z.at[some_norm], norm_z.at[some_norm], norm_sem.at[0], norm_sem.at[1], seq_at(me)
    ).wait_recv()
    total = jnp.zeros((2, 128), F32)
    for z in range(SIDE):
        at = pl.ds(my_y * SIDE + z, 1)
        total = a_rows[at, :] * total + b_rows[at, :] * norm_z[z]
    norm_y[my_y] = total
    for step in range(1, rows):
        remote(
            norm_y.at[my_y], norm_y.at[my_y], norm_sem.at[2], norm_sem.at[3], seq_at(y_peer(step))
        ).start()

    m_in = m_rows[pl.ds(me, 1), :][:, 0:1]
    begin_full = jnp.concatenate([begin_col] * (tokens // 128), axis=1)
    allowed = (s_full <= t_full) & (s_full >= begin_full)
    log_weight = jnp.where(allowed, gain_row + cum_col, NEG)
    carried = jnp.where(begin_col[:, 0:1] < 0, m_in + cum_col, NEG)
    row_max = jnp.maximum(jnp.max(log_weight, axis=1, keepdims=True), carried)
    weights = scores * jnp.exp(log_weight - row_max)
    reach = jnp.exp(carried - row_max) * scale
    num_ref[...] = jnp.dot(weights.astype(BF16), value, preferred_element_type=F32)
    den_inside = jnp.sum(weights, axis=1, keepdims=True)

    most_tiles = pl.ds(0, shards - 1)
    remote(
        got_tiles.at[most_tiles],
        got_tiles.at[most_tiles],
        tile_sem.at[0],
        tile_sem.at[1],
        seq_at(me),
    ).wait_recv()
    state = jnp.zeros((16, 128), F32)
    for s in range(shards):
        back_tiles[s] = state.astype(BF16)
        state = a_rows[s : s + 1, :] * state + b_rows[s : s + 1, :] * got_tiles[s].astype(F32)

    def send_back(step, carry):
        peer = (me + step) % shards
        remote(
            back_tiles.at[peer], mem_tiles.at[me], tile_sem.at[2], tile_sem.at[3], seq_at(peer)
        ).start()
        return carry

    lax.fori_loop(1, shards, send_back, 0)
    mem_tiles[me] = back_tiles[me]

    some_y = pl.ds(0, rows - 1)
    remote(
        norm_y.at[some_y], norm_y.at[some_y], norm_sem.at[2], norm_sem.at[3], seq_at(me)
    ).wait_recv()
    norm_in = jnp.zeros((2, 128), F32)
    for y in range(rows):
        decay = a_rows[y * SIDE : y * SIDE + 1, :]
        for z in range(1, SIDE):
            decay = decay * a_rows[y * SIDE + z : y * SIDE + z + 1, :]
        norm_in = jnp.where(y < my_y, decay * norm_in + norm_y[y], norm_in)
    for z in range(SIDE):
        at = pl.ds(my_y * SIDE + z, 1)
        norm_in = jnp.where(
            z < my_z, a_rows[at, :] * norm_in + b_rows[at, :] * norm_z[z], norm_in
        )
    norm_row = jnp.concatenate([norm_in[0:1, :], norm_in[1:2, :]], axis=1)
    from_normal = jnp.sum(query.astype(F32) * norm_row, axis=1, keepdims=True)
    floor = jnp.maximum(jnp.abs(den_inside + reach * from_normal), 1.0)
    inverse = 1.0 / floor

    wo_copy.wait()
    remote(
        mem_tiles.at[most_tiles],
        mem_tiles.at[most_tiles],
        tile_sem.at[2],
        tile_sem.at[3],
        seq_at(me),
    ).wait_recv()
    parts = []
    for c in range(values // 128):
        block = mem_tiles[c * tile_rows : (c + 1) * tile_rows].reshape(width, 128)
        from_memory = jnp.dot(query, block, preferred_element_type=F32)
        at = slice(c * 128, (c + 1) * 128)
        parts.append(((num_ref[:, at] + reach * from_memory) * inverse).astype(BF16))
    head_out = jnp.concatenate(parts, axis=1)

    out_cols = out_ref.shape[1]

    def project(x, core):
        column = pl.multiple_of((2 * x + core) * out_cols, out_cols)
        return jnp.dot(head_out, wo_ref[:, pl.ds(column, out_cols)], preferred_element_type=F32)

    order = [1, 2, 3, 0] if chips == 4 else list(range(1, chips)) + [0]
    pair_copies = {}
    for step in order:
        pair_send[step] = project((my_x + step) % chips, 1 - my_c).astype(BF16)
        pair_copies[step] = remote(
            pair_send.at[step],
            pair_recv.at[step],
            pair_ssem.at[step],
            pair_rsem.at[step],
            head_at(partner),
        )
        pair_copies[step].start()
    x_copies = []
    for step in order:
        ours = project((my_x + step) % chips, my_c)
        pair_copies[step].wait_recv()
        both = ours + pair_recv[step].astype(F32)
        if step:
            x_send[step - 1] = both.astype(BF16)
            copy = remote(
                x_send.at[step - 1],
                x_recv.at[step - 1],
                x_ssem.at[step - 1],
                x_rsem.at[step - 1],
                head_at(2 * ((my_x + step) % chips) + my_c),
            )
            copy.start()
            x_copies.append(copy)
    for step, copy in enumerate(x_copies):
        copy.wait_recv()
        both = both + x_recv[step].astype(F32)
    out_ref[...] = both.astype(BF16)

    halo.wait_send()
    remote(
        scal_ref.at[some], scal_ref.at[some], scal_sem.at[0], scal_sem.at[1], seq_at(me)
    ).wait_send()
    remote(
        scal_ref.at[most], scal_ref.at[most], scal_sem.at[2], scal_sem.at[3], seq_at(me)
    ).wait_send()
    remote(
        norm_z.at[some_norm], norm_z.at[some_norm], norm_sem.at[0], norm_sem.at[1], seq_at(me)
    ).wait_send()
    remote(
        norm_y.at[some_y], norm_y.at[some_y], norm_sem.at[2], norm_sem.at[3], seq_at(me)
    ).wait_send()
    for first, tiles in ((0, own_tiles), (2, back_tiles)):
        remote(
            tiles.at[most_tiles],
            tiles.at[most_tiles],
            tile_sem.at[first],
            tile_sem.at[first + 1],
            seq_at(me),
        ).wait_send()
    for copy in list(pair_copies.values()) + x_copies:
        copy.wait_send()


def on_device(
    shards,
    chips,
    query_input,
    key_input,
    value_input,
    kernel_taps,
    input_gate,
    forget_gate,
    request_lengths,
    output_weight,
):
    tokens, width = query_input.shape
    values = value_input.shape[1]
    out_cols = output_weight.shape[1] // (2 * chips)
    vmem = pl.BlockSpec(memory_space=pltpu.VMEM)
    dma = pltpu.SemaphoreType.DMA
    return pl.pallas_call(
        functools.partial(kernel, shards, chips),
        out_shape=jax.ShapeDtypeStruct((tokens, out_cols), BF16),
        in_specs=[pl.BlockSpec(memory_space=pltpu.SMEM)]
        + [vmem] * 6
        + [pl.BlockSpec(memory_space=pl.ANY)],
        out_specs=vmem,
        scratch_shapes=[
            pltpu.VMEM(output_weight.shape, BF16),
            pltpu.VMEM((tokens + 8, width), F32),
            pltpu.VMEM((2, 16, width), BF16),
            pltpu.VMEM((2, 16, width), BF16),
            pltpu.VMEM((shards, 2, 128), F32),
            pltpu.VMEM((shards, 128), F32),
            pltpu.VMEM((shards, 128), F32),
            pltpu.VMEM((shards, 128), F32),
            pltpu.VMEM((shards, 128), F32),
            pltpu.VMEM((shards, 128), F32),
            pltpu.VMEM((shards, 16, 128), BF16),
            pltpu.VMEM((shards, 16, 128), BF16),
            pltpu.VMEM((shards, 16, 128), BF16),
            pltpu.VMEM((shards, 16, 128), BF16),
            pltpu.VMEM((SIDE, 2, 128), F32),
            pltpu.VMEM((shards // SIDE, 2, 128), F32),
            pltpu.VMEM((tokens, values), F32),
            pltpu.VMEM((chips, tokens, out_cols), BF16),
            pltpu.VMEM((chips, tokens, out_cols), BF16),
            pltpu.VMEM((chips - 1, tokens, out_cols), BF16),
            pltpu.VMEM((chips - 1, tokens, out_cols), BF16),
            dma,
            dma((2,)),
            dma((4,)),
            dma((4,)),
            dma((4,)),
            dma((chips,)),
            dma((chips,)),
            dma((chips - 1,)),
            dma((chips - 1,)),
        ],
        compiler_params=pltpu.CompilerParams(
            collective_id=0, has_side_effects=True, vmem_limit_bytes=40 << 20
        ),
    )(
        request_lengths,
        query_input,
        key_input,
        value_input,
        kernel_taps,
        input_gate,
        forget_gate,
        output_weight,
    )


def solution(mesh):
    placed = (
        P("seq", "head"),
        P("seq", "head"),
        P("seq", "head"),
        P(None, None, "head"),
        P("head", "seq"),
        P("head", "seq"),
        P(),
        P("head", None),
    )
    return jax.shard_map(
        functools.partial(on_device, mesh.shape["seq"], mesh.shape["head"] // 2),
        mesh=mesh,
        in_specs=placed,
        out_specs=P("seq", "head"),
        check_vma=False,
    )
```

time: 553 us -> 63.5 us (0.11)
  the two profiles are of different devices: /device:TPU:8 before, /device:TPU:1 now
where the time goes in v1:
time: 63.5 us; the launch traced here: 63.2 us
  Pallas kernels  55.4 us (87%)
  local copies, waits for them, and re-layouts  7.71 us (12%)
    pallas_call x1, Pallas kernels, on_device(): pl.pallas_call(functools.partial(kernel, shards, chips), out_shape=jax.Sh...  55.4 us
    unnamed x17, local copies, waits for them, and re-layouts  7.71 us

profile of v1, /device:TPU:1, one launch (start us, length us, event | category | flops | bytes accessed | tf_op | source)
XLA Modules:
  0.0 63.2 jit_solution(355830084610403717)
XLA Ops:
  0.0 0.0 copy-start
  0.0 1.6 %copy-done = bf16[512,2048]{1,0:T(8,128)(2,1)S(1)} copy-done((bf16[512,2048]{1,0:T(8,128)(2,1)S(1)}, bf16[512,2048]{1,0:T(8,128)(2,1)}, u32[]{:S(2)}) %copy-start) | copy-done | bytes 2097176
  1.6 0.0 copy-start.1
  1.6 0.9 %copy-done.1 = bf16[256,512]{1,0:T(8,128)(2,1)S(1)} copy-done((bf16[256,512]{1,0:T(8,128)(2,1)S(1)}, bf16[256,512]{1,0:T(8,128)(2,1)}, u32[]{:S(2)}) %copy-start.1) | copy-done | bytes 262168
  2.5 0.0 copy-start.2
  2.5 0.9 %copy-done.2 = bf16[256,256]{1,0:T(8,128)(2,1)S(1)} copy-done((bf16[256,256]{1,0:T(8,128)(2,1)S(1)}, bf16[256,256]{1,0:T(8,128)(2,1)}, u32[]{:S(2)}) %copy-start.2) | copy-done | bytes 131096
  3.4 0.0 copy-start.3
  3.4 0.9 %copy-done.3 = bf16[256,256]{1,0:T(8,128)(2,1)S(1)} copy-done((bf16[256,256]{1,0:T(8,128)(2,1)S(1)}, bf16[256,256]{1,0:T(8,128)(2,1)}, u32[]{:S(2)}) %copy-start.3) | copy-done | bytes 131096
  4.4 0.0 copy-start.4
  4.4 0.7 %copy-done.4 = f32[2,4,256]{2,1,0:T(4,128)S(1)} copy-done((f32[2,4,256]{2,1,0:T(4,128)S(1)}, f32[2,4,256]{2,1,0:T(4,128)}, u32[]{:S(2)}) %copy-start.4) | copy-done | bytes 8216
  5.0 0.0 copy-start.5
  5.1 0.7 %copy-done.5 = f32[1,256]{1,0:T(1,128)S(1)} copy-done((f32[1,256]{1,0:T(1,128)S(1)}, f32[1,256]{1,0:T(1,128)}, u32[]{:S(2)}) %copy-start.5) | copy-done | bytes 1048
  5.7 0.0 copy-start.6
  5.7 0.7 %copy-done.6 = f32[1,256]{1,0:T(1,128)S(1)} copy-done((f32[1,256]{1,0:T(1,128)S(1)}, f32[1,256]{1,0:T(1,128)}, u32[]{:S(2)}) %copy-start.6) | copy-done | bytes 1048
  6.4 0.0 copy-start.7
  6.4 0.7 %copy-done.7 = s32[4]{0:T(128)S(1)} copy-done((s32[4]{0:T(128)S(1)}, s32[4]{0:T(128)}, u32[]{:S(2)}) %copy-start.7) | copy-done | bytes 40
  7.1 55.4 %shard_map.82 = bf16[256,256]{1,0:T(8,128)(2,1)S(1)} custom-call(s32[4]{0:T(128)S(1)} %copy-done.7, bf16[256,256]{1,0:T(8,128)(2,1)S(1)} %copy-done.2, bf16[256,256]{1,0:T(8,128)(2,1)S(1)} %copy-done.3, bf16[256,512]{1,0:T(8,128)(2,1)S(1)} %copy-done.1, f32[2,4,256]{2,1,0:T(4,128)S(1)} %copy-done.4, f32[1,256]{1,0:T(1,128)S(1)} %copy-done.5, ...), custom_call_target="tpu_custom_call" | custom-call | tf_op jit(solution)/shard_map/pallas_call | solution.py:412
  62.5 0.7 %copy.10 = bf16[256,256]{1,0:T(8,128)(2,1)} copy(bf16[256,256]{1,0:T(8,128)(2,1)S(1)} %shard_map.82) | data formatting | bytes 262144
Async XLA Ops:
  0.0 1.6 %copy-start = (bf16[512,2048]{1,0:T(8,128)(2,1)S(1)}, bf16[512,2048]{1,0:T(8,128)(2,1)}, u32[]{:S(2)}) copy-start(bf16[512,2048]{1,0:T(8,128)(2,1)} %wo_hbm.1) | copy-start | bytes 6291460
  1.6 0.9 %copy-start.1 = (bf16[256,512]{1,0:T(8,128)(2,1)S(1)}, bf16[256,512]{1,0:T(8,128)(2,1)}, u32[]{:S(2)}) copy-start(bf16[256,512]{1,0:T(8,128)(2,1)} %v_ref.1) | copy-start | bytes 786436
  2.5 0.9 %copy-start.2 = (bf16[256,256]{1,0:T(8,128)(2,1)S(1)}, bf16[256,256]{1,0:T(8,128)(2,1)}, u32[]{:S(2)}) copy-start(bf16[256,256]{1,0:T(8,128)(2,1)} %q_ref.1) | copy-start | bytes 393220
  3.4 0.9 %copy-start.3 = (bf16[256,256]{1,0:T(8,128)(2,1)S(1)}, bf16[256,256]{1,0:T(8,128)(2,1)}, u32[]{:S(2)}) copy-start(bf16[256,256]{1,0:T(8,128)(2,1)} %k_ref.1) | copy-start | bytes 393220
  4.4 0.7 %copy-start.4 = (f32[2,4,256]{2,1,0:T(4,128)S(1)}, f32[2,4,256]{2,1,0:T(4,128)}, u32[]{:S(2)}) copy-start(f32[2,4,256]{2,1,0:T(4,128)} %taps_ref.1) | copy-start | bytes 24580
  5.0 0.7 %copy-start.5 = (f32[1,256]{1,0:T(1,128)S(1)}, f32[1,256]{1,0:T(1,128)}, u32[]{:S(2)}) copy-start(f32[1,256]{1,0:T(1,128)} %ig_ref.1) | copy-start | bytes 3076
  5.7 0.7 %copy-start.6 = (f32[1,256]{1,0:T(1,128)S(1)}, f32[1,256]{1,0:T(1,128)}, u32[]{:S(2)}) copy-start(f32[1,256]{1,0:T(1,128)} %fg_ref.1) | copy-start | bytes 3076
  6.4 0.7 %copy-start.7 = (s32[4]{0:T(128)S(1)}, s32[4]{0:T(128)}, u32[]{:S(2)}) copy-start(s32[4]{0:T(128)} %len_ref.1) | copy-start | bytes 52

commit v2 on v1

--- a/solution.py
+++ b/solution.py
@@ -17,6 +17,15 @@
 def kernel(
     shards,
     chips,
+    len_hbm,
+    q_hbm,
+    k_hbm,
+    v_hbm,
+    taps_hbm,
+    ig_hbm,
+    fg_hbm,
+    wo_hbm,
+    out_ref,
     len_ref,
     q_ref,
     k_ref,
@@ -24,11 +33,8 @@
     taps_ref,
     ig_ref,
     fg_ref,
-    wo_hbm,
-    out_ref,
     wo_ref,
     ext_ref,
-    halo_send,
     halo_recv,
     scal_ref,
     stab_rows,
@@ -47,7 +53,7 @@
     pair_recv,
     x_send,
     x_recv,
-    wo_sem,
+    load_sem,
     halo_sem,
     scal_sem,
     norm_sem,
@@ -56,9 +62,10 @@
     pair_rsem,
     x_ssem,
     x_rsem,
+    rows_sem,
 ):
-    tokens, width = q_ref.shape
-    values = v_ref.shape[1]
+    tokens, width = q_hbm.shape
+    values = v_hbm.shape[1]
     scale = 1.0 / (width**0.5)
     me = lax.axis_index("seq")
     head = lax.axis_index("head")
@@ -77,28 +84,43 @@
             src_ref=src, dst_ref=dst, send_sem=ssem, recv_sem=rsem, device_id=where, device_id_type=MESH
         )
 
-    wo_copy = pltpu.make_async_copy(wo_hbm, wo_ref, wo_sem)
-    wo_copy.start()
+    loads = [
+        pltpu.make_async_copy(src, dst, load_sem.at[i])
+        for i, (src, dst) in enumerate(
+            (
+                (fg_hbm, fg_ref),
+                (ig_hbm, ig_ref),
+                (k_hbm, k_ref),
+                (q_hbm, q_ref),
+                (taps_hbm, taps_ref),
+                (v_hbm, v_ref),
+                (wo_hbm, wo_ref),
+                (len_hbm, len_ref),
+            )
+        )
+    ]
+    for load in loads:
+        load.start()
 
     barrier = pltpu.get_barrier_semaphore()
 
-    def greet(step, carry):
-        pl.semaphore_signal(
-            barrier, inc=1, device_id=seq_at((me + step) % shards), device_id_type=MESH
-        )
-        return carry
-
-    lax.fori_loop(1, shards, greet, 0)
+    def z_peer(step):
+        return my_y * SIDE + (my_z + step) % SIDE
+
+    def y_peer(step):
+        return ((my_y + step) % rows) * SIDE + my_z
+
     partner = 2 * my_x + (1 - my_c)
-    pl.semaphore_signal(barrier, inc=1, device_id=head_at(partner), device_id_type=MESH)
-    for step in range(1, chips):
-        pl.semaphore_signal(
-            barrier,
-            inc=1,
-            device_id=head_at(2 * ((my_x + step) % chips) + my_c),
-            device_id_type=MESH,
-        )
-
+    x_next = 2 * ((my_x + 1) % chips) + my_c
+    x_prev = 2 * ((my_x + chips - 1) % chips) + my_c
+    known = [seq_at((me + shards - 1) % shards)]
+    known += [seq_at(z_peer(step)) for step in (4, 3, 5, 2, 6, 1, 7)]
+    known += [seq_at(y_peer(step)) for step in (4, 3, 5, 2, 6, 1, 7)]
+    known += [head_at(partner), head_at(x_next), head_at(x_prev)]
+    for where in known:
+        pl.semaphore_signal(barrier, inc=1, device_id=where, device_id_type=MESH)
+
+    loads[7].wait()
     offset = me * tokens
     starts = [jnp.int32(0)]
     for r in range(len_ref.shape[0] - 1):
@@ -118,6 +140,8 @@
         last_begin = jnp.where(start <= offset + (tokens - 1), start, last_begin)
     last_begin = last_begin - offset
 
+    loads[0].wait()
+    loads[1].wait()
     fg = fg_ref[...]
     ig = ig_ref[...]
     log_forget = -(jnp.maximum(-fg, 0.0) + jnp.log1p(jnp.exp(-jnp.abs(fg))))
@@ -149,59 +173,83 @@
     cum_col = turned[:, 0:1]
     factor_col = turned[:, 1:2]
 
-    halo_send[0] = k_ref[tokens - 16 : tokens, :]
-    halo_send[1] = q_ref[tokens - 16 : tokens, :]
-
-    pl.semaphore_wait(barrier, shards - 1 + chips)
-
-    halo = remote(
-        halo_send, halo_recv, halo_sem.at[0], halo_sem.at[1], seq_at((me + 1) % shards)
-    )
-    halo.start()
-
-    def z_peer(step):
-        return my_y * SIDE + (my_z + step) % SIDE
-
-    def y_peer(step):
-        return ((my_y + step) % rows) * SIDE + my_z
-
-    for step in range(1, SIDE):
+    loads[2].wait()
+    loads[3].wait()
+    pl.semaphore_wait(barrier, len(known))
+
+    tail = pl.ds(tokens - 16, 16)
+    follower = seq_at((me + 1) % shards)
+    halos = [
+        remote(ref.at[tail, :], halo_recv.at[i], halo_sem.at[2 * i], halo_sem.at[2 * i + 1], follower)
+        for i, ref in enumerate((k_ref, q_ref))
+    ]
+    halos[0].start()
+    for step in (4, 3, 5, 2, 6, 1, 7):
+        pl.semaphore_signal(
+            rows_sem, inc=1, device_id=seq_at(y_peer(step)), device_id_type=MESH
+        )
+    for step in (4, 3, 5, 2, 6, 1, 7):
         remote(
             scal_ref.at[me], scal_ref.at[me], scal_sem.at[0], scal_sem.at[1], seq_at(z_peer(step))
         ).start()
-
-    def conv_silu(source, which, tail):
-        ext_ref[0:8, :] = halo_recv[tail, 8:16, :].astype(F32)
-        ext_ref[8 : 8 + tokens, :] = source[...].astype(F32)
-        running = taps_ref[which, 0:1, :] * ext_ref[8 : 8 + tokens, :]
+    halos[1].start()
+
+    def conv_silu(which, first, count):
+        begin = begin_col[first : first + count]
+        position = t_col[first : first + count]
+        running = taps_ref[which, 0:1, :] * ext_ref[8 + first : 8 + first + count, :]
         for lag in range(1, taps_ref.shape[1]):
-            keep = (t_col - lag) >= begin_col
+            keep = (position - lag) >= begin
             keep = jnp.concatenate([keep.astype(F32)] * (width // 128), axis=1) > 0.0
-            shifted = ext_ref[8 - lag : 8 - lag + tokens, :]
+            shifted = ext_ref[8 + first - lag : 8 + first - lag + count, :]
             running = running + jnp.where(keep, taps_ref[which, lag : lag + 1, :] * shifted, 0.0)
         return (running / (1.0 + jnp.exp(-running))).astype(BF16)
 
-    halo.wait_recv()
-    key = conv_silu(k_ref, 1, 0)
-    weighted = key.astype(F32) * factor_col
+    def outer_sum(left, right):
+        return lax.dot_general(
+            left, right, (((0,), (0,)), ((), ())), preferred_element_type=F32
+        )
+
+    loads[4].wait()
+    loads[5].wait()
+    ext_ref[8 : 8 + tokens, :] = k_ref[...].astype(F32)
+    key_rest = conv_silu(1, 16, tokens - 16)
+    weighted_rest = key_rest.astype(F32) * factor_col[16:]
+    memory_rest = outer_sum(weighted_rest.astype(BF16), v_ref[16:, :])
+    normal_rest = jnp.sum(weighted_rest, axis=0, keepdims=True)
+    halos[0].wait_recv()
+    ext_ref[0:8, :] = halo_recv[0, 8:16, :].astype(F32)
+    key_first = conv_silu(1, 0, 16)
+    weighted_first = key_first.astype(F32) * factor_col[:16]
+    memory = (memory_rest + outer_sum(weighted_first.astype(BF16), v_ref[:16, :])).astype(BF16)
+    key = jnp.concatenate([key_first, key_rest], axis=0)
     value = v_ref[...]
-    memory = lax.dot_general(
-        weighted.astype(BF16), value, (((0,), (0,)), ((), ())), preferred_element_type=F32
-    ).astype(BF16)
     tile_rows = width // 16
     for c in range(values // 128):
         own_tiles[c * tile_rows : (c + 1) * tile_rows] = memory[
             :, c * 128 : (c + 1) * 128
         ].reshape(tile_rows, 16, 128)
-    normal = jnp.sum(weighted, axis=0, keepdims=True)
+    normal = normal_rest + jnp.sum(weighted_first, axis=0, keepdims=True)
     norm_z[my_z] = jnp.concatenate([normal[:, 0:128], normal[:, 128:256]], axis=0)
 
-    def send_tile(step, carry):
-        peer = (me + step) % shards
-        remote(
-            own_tiles.at[peer], got_tiles.at[me], tile_sem.at[0], tile_sem.at[1], seq_at(peer)
-        ).start()
-        return carry
+    def far(step):
+        dy, dz = step // SIDE, step % SIDE
+        return -(min(dy, rows - dy) + min(dz, SIDE - dz))
+
+    steps = sorted(range(1, shards), key=far)
+
+    def peer_at(step):
+        return ((my_y + step // SIDE) % rows) * SIDE + (my_z + step % SIDE) % SIDE
+
+    def send_tiles(chosen):
+        for step in chosen:
+            peer = peer_at(step)
+            remote(
+                own_tiles.at[peer], got_tiles.at[me], tile_sem.at[0], tile_sem.at[1], seq_at(peer)
+            ).start()
+
+    pl.semaphore_wait(rows_sem, rows - 1)
+    send_tiles(steps[:24])
 
     some = pl.ds(0, SIDE - 1)
     remote(
@@ -216,14 +264,17 @@
             scal_sem.at[3],
             seq_at(y_peer(step)),
         ).start()
-    lax.fori_loop(1, shards, send_tile, 0)
+    send_tiles(steps[24:])
     for step in range(1, SIDE):
         remote(
             norm_z.at[my_z], norm_z.at[my_z], norm_sem.at[0], norm_sem.at[1], seq_at(z_peer(step))
         ).start()
     got_tiles[me] = own_tiles[me]
 
-    query = conv_silu(q_ref, 0, 1)
+    halos[1].wait_recv()
+    ext_ref[0:8, :] = halo_recv[1, 8:16, :].astype(F32)
+    ext_ref[8 : 8 + tokens, :] = q_ref[...].astype(F32)
+    query = conv_silu(0, 0, tokens)
     scores = (
         lax.dot_general(query, key, (((1,), (1,)), ((), ())), preferred_element_type=F32) * scale
     )
@@ -282,14 +333,11 @@
         back_tiles[s] = state.astype(BF16)
         state = a_rows[s : s + 1, :] * state + b_rows[s : s + 1, :] * got_tiles[s].astype(F32)
 
-    def send_back(step, carry):
-        peer = (me + step) % shards
+    for step in steps:
+        peer = peer_at(step)
         remote(
             back_tiles.at[peer], mem_tiles.at[me], tile_sem.at[2], tile_sem.at[3], seq_at(peer)
         ).start()
-        return carry
-
-    lax.fori_loop(1, shards, send_back, 0)
     mem_tiles[me] = back_tiles[me]
 
     some_y = pl.ds(0, rows - 1)
@@ -312,7 +360,7 @@
     floor = jnp.maximum(jnp.abs(den_inside + reach * from_normal), 1.0)
     inverse = 1.0 / floor
 
-    wo_copy.wait()
+    loads[6].wait()
     remote(
         mem_tiles.at[most_tiles],
         mem_tiles.at[most_tiles],
@@ -329,14 +377,15 @@
     head_out = jnp.concatenate(parts, axis=1)
 
     out_cols = out_ref.shape[1]
+    half = tokens // 2
 
     def project(x, core):
         column = pl.multiple_of((2 * x + core) * out_cols, out_cols)
         return jnp.dot(head_out, wo_ref[:, pl.ds(column, out_cols)], preferred_element_type=F32)
 
-    order = [1, 2, 3, 0] if chips == 4 else list(range(1, chips)) + [0]
     pair_copies = {}
-    for step in order:
+
+    def pair_start(step):
         pair_send[step] = project((my_x + step) % chips, 1 - my_c).astype(BF16)
         pair_copies[step] = remote(
             pair_send.at[step],
@@ -346,28 +395,49 @@
             head_at(partner),
         )
         pair_copies[step].start()
-    x_copies = []
-    for step in order:
+
+    def chip_sum(step):
         ours = project((my_x + step) % chips, my_c)
         pair_copies[step].wait_recv()
-        both = ours + pair_recv[step].astype(F32)
-        if step:
-            x_send[step - 1] = both.astype(BF16)
-            copy = remote(
-                x_send.at[step - 1],
-                x_recv.at[step - 1],
-                x_ssem.at[step - 1],
-                x_rsem.at[step - 1],
-                head_at(2 * ((my_x + step) % chips) + my_c),
-            )
-            copy.start()
-            x_copies.append(copy)
-    for step, copy in enumerate(x_copies):
-        copy.wait_recv()
-        both = both + x_recv[step].astype(F32)
-    out_ref[...] = both.astype(BF16)
-
-    halo.wait_send()
+        return ours + pair_recv[step].astype(F32)
+
+    def x_copy(slot, where):
+        return remote(
+            x_send.at[slot], x_recv.at[slot], x_ssem.at[slot], x_rsem.at[slot], head_at(where)
+        )
+
+    x_copies = [x_copy(slot, x_next if slot % 2 == 0 else x_prev) for slot in range(6)]
+    pair_start(2)
+    pair_start(1)
+    pair_start(3)
+    pair_start(0)
+    opposite = chip_sum(2)
+    x_send[0] = opposite[:half].astype(BF16)
+    x_copies[0].start()
+    x_send[1] = opposite[half:].astype(BF16)
+    x_copies[1].start()
+    after = chip_sum(1)
+    x_send[2] = after[half:].astype(BF16)
+    x_copies[2].start()
+    before = chip_sum(3)
+    x_send[3] = before[:half].astype(BF16)
+    x_copies[3].start()
+    x_copies[0].wait_recv()
+    x_send[4] = (after[:half] + x_recv[0].astype(F32)).astype(BF16)
+    x_copies[4].start()
+    x_copies[1].wait_recv()
+    x_send[5] = (before[half:] + x_recv[1].astype(F32)).astype(BF16)
+    x_copies[5].start()
+    both = chip_sum(0)
+    x_copies[3].wait_recv()
+    x_copies[4].wait_recv()
+    out_ref[:half] = (both[:half] + x_recv[3].astype(F32) + x_recv[4].astype(F32)).astype(BF16)
+    x_copies[2].wait_recv()
+    x_copies[5].wait_recv()
+    out_ref[half:] = (both[half:] + x_recv[2].astype(F32) + x_recv[5].astype(F32)).astype(BF16)
+
+    for copy in halos:
+        copy.wait_send()
     remote(
         scal_ref.at[some], scal_ref.at[some], scal_sem.at[0], scal_sem.at[1], seq_at(me)
     ).wait_send()
@@ -412,14 +482,23 @@
     return pl.pallas_call(
         functools.partial(kernel, shards, chips),
         out_shape=jax.ShapeDtypeStruct((tokens, out_cols), BF16),
-        in_specs=[pl.BlockSpec(memory_space=pltpu.SMEM)]
-        + [vmem] * 6
-        + [pl.BlockSpec(memory_space=pl.ANY)],
+        in_specs=[pl.BlockSpec(memory_space=pltpu.HBM)] * 8,
         out_specs=vmem,
-        scratch_shapes=[
+        scratch_shapes=[pltpu.SMEM(request_lengths.shape, jnp.int32)]
+        + [
+            pltpu.VMEM(a.shape, a.dtype)
+            for a in (
+                query_input,
+                key_input,
+                value_input,
+                kernel_taps,
+                input_gate,
+                forget_gate,
+            )
+        ]
+        + [
             pltpu.VMEM(output_weight.shape, BF16),
             pltpu.VMEM((tokens + 8, width), F32),
-            pltpu.VMEM((2, 16, width), BF16),
             pltpu.VMEM((2, 16, width), BF16),
             pltpu.VMEM((shards, 2, 128), F32),
             pltpu.VMEM((shards, 128), F32),
@@ -436,30 +515,36 @@
             pltpu.VMEM((tokens, values), F32),
             pltpu.VMEM((chips, tokens, out_cols), BF16),
             pltpu.VMEM((chips, tokens, out_cols), BF16),
-            pltpu.VMEM((chips - 1, tokens, out_cols), BF16),
-            pltpu.VMEM((chips - 1, tokens, out_cols), BF16),
-            dma,
-            dma((2,)),
+            pltpu.VMEM((6, tokens // 2, out_cols), BF16),
+            pltpu.VMEM((6, tokens // 2, out_cols), BF16),
+            dma((8,)),
+            dma((4,)),
             dma((4,)),
             dma((4,)),
             dma((4,)),
             dma((chips,)),
             dma((chips,)),
-            dma((chips - 1,)),
-            dma((chips - 1,)),
+            dma((6,)),
+            dma((6,)),
+            pltpu.SemaphoreType.REGULAR,
         ],
         compiler_params=pltpu.CompilerParams(
-            collective_id=0, has_side_effects=True, vmem_limit_bytes=40 << 20
+            collective_id=0, has_side_effects=True, vmem_limit_bytes=32 << 20
         ),
     )(
-        request_lengths,
-        query_input,
-        key_input,
-        value_input,
-        kernel_taps,
-        input_gate,
-        forget_gate,
-        output_weight,
+        *(
+            pltpu.with_memory_space_constraint(a, pltpu.HBM)
+            for a in (
+                request_lengths,
+                query_input,
+                key_input,
+                value_input,
+                kernel_taps,
+                input_gate,
+                forget_gate,
+                output_weight,
+            )
+        ),
     )
 
 

time: 63.5 us -> 46.4 us (0.73)
  Pallas kernels: 55.4 us -> 45.6 us
  local copies, waits for them, and re-layouts: 7.71 us -> 0.66 us
    pallas_call x1, Pallas kernels: 55.4 us -> 45.6 us  [on_device(): pl.pallas_call(functools.partial(kernel, shards, chips), out_shape=jax.Sh...]
    unnamed x17 -> x1, local copies, waits for them, and re-layouts: 7.71 us -> 0.66 us
where the time goes in v2:
time: 46.4 us; the launch traced here: 46.3 us
  Pallas kernels  45.6 us (98%)
  local copies, waits for them, and re-layouts  0.66 us (1%)
    pallas_call x1, Pallas kernels, on_device(): pl.pallas_call(functools.partial(kernel, shards, chips), out_shape=jax.Sh...  45.6 us

profile of v2, /device:TPU:1, one launch (start us, length us, event | category | flops | bytes accessed | tf_op | source)
XLA Modules:
  0.0 46.3 jit_solution(13208461141653972773)
XLA Ops:
  0.0 45.6 %shard_map.82 = bf16[256,256]{1,0:T(8,128)(2,1)S(1)} custom-call(s32[4]{0:T(128)} %len_hbm.1, bf16[256,256]{1,0:T(8,128)(2,1)} %q_hbm.1, bf16[256,256]{1,0:T(8,128)(2,1)} %k_hbm.1, bf16[256,512]{1,0:T(8,128)(2,1)} %v_hbm.1, f32[2,4,256]{2,1,0:T(4,128)} %taps_hbm.1, f32[1,256]{1,0:T(1,128)} %ig_hbm.1, f32[1,256]{1,0:T(1,128)} %fg_hbm.1, bf16[512,2048]{1,0:T(8,128)(2,1)} %wo_hbm.1), custom_call_target="tpu_custom_call" | custom-call | tf_op jit(solution)/shard_map/pallas_call | solution.py:482
  45.6 0.7 %copy.10 = bf16[256,256]{1,0:T(8,128)(2,1)} copy(bf16[256,256]{1,0:T(8,128)(2,1)S(1)} %shard_map.82) | data formatting | bytes 262144

commit v3 on v2

--- a/solution.py
+++ b/solution.py
@@ -84,6 +84,24 @@
             src_ref=src, dst_ref=dst, send_sem=ssem, recv_sem=rsem, device_id=where, device_id_type=MESH
         )
 
+    barrier = pltpu.get_barrier_semaphore()
+
+    def z_peer(step):
+        return my_y * SIDE + (my_z + step) % SIDE
+
+    def y_peer(step):
+        return ((my_y + step) % rows) * SIDE + my_z
+
+    partner = 2 * my_x + (1 - my_c)
+    x_next = 2 * ((my_x + 1) % chips) + my_c
+    x_prev = 2 * ((my_x + chips - 1) % chips) + my_c
+    known = [seq_at((me + shards - 1) % shards)]
+    known += [seq_at(z_peer(step)) for step in (4, 3, 5, 2, 6, 1, 7)]
+    known += [seq_at(y_peer(step)) for step in (4, 3, 5, 2, 6, 1, 7)]
+    known += [head_at(partner), head_at(x_next), head_at(x_prev)]
+    for where in known:
+        pl.semaphore_signal(barrier, inc=1, device_id=where, device_id_type=MESH)
+
     loads = [
         pltpu.make_async_copy(src, dst, load_sem.at[i])
         for i, (src, dst) in enumerate(
@@ -101,24 +119,6 @@
     ]
     for load in loads:
         load.start()
-
-    barrier = pltpu.get_barrier_semaphore()
-
-    def z_peer(step):
-        return my_y * SIDE + (my_z + step) % SIDE
-
-    def y_peer(step):
-        return ((my_y + step) % rows) * SIDE + my_z
-
-    partner = 2 * my_x + (1 - my_c)
-    x_next = 2 * ((my_x + 1) % chips) + my_c
-    x_prev = 2 * ((my_x + chips - 1) % chips) + my_c
-    known = [seq_at((me + shards - 1) % shards)]
-    known += [seq_at(z_peer(step)) for step in (4, 3, 5, 2, 6, 1, 7)]
-    known += [seq_at(y_peer(step)) for step in (4, 3, 5, 2, 6, 1, 7)]
-    known += [head_at(partner), head_at(x_next), head_at(x_prev)]
-    for where in known:
-        pl.semaphore_signal(barrier, inc=1, device_id=where, device_id_type=MESH)
 
     loads[7].wait()
     offset = me * tokens
@@ -295,6 +295,14 @@
     a_rows[...] = jnp.exp(thr_rows[...])
     b_rows[...] = jnp.exp(stab_rows[...])
 
+    most_tiles = pl.ds(0, shards - 1)
+    remote(
+        got_tiles.at[most_tiles],
+        got_tiles.at[most_tiles],
+        tile_sem.at[0],
+        tile_sem.at[1],
+        seq_at(me),
+    ).wait_recv()
     some_norm = pl.ds(0, SIDE - 1)
     remote(
         norm_z.at[some_norm], norm_z.at[some_norm], norm_sem.at[0], norm_sem.at[1], seq_at(me)
@@ -309,6 +317,25 @@
             norm_y.at[my_y], norm_y.at[my_y], norm_sem.at[2], norm_sem.at[3], seq_at(y_peer(step))
         ).start()
 
+    state = jnp.zeros((16, 128), F32)
+    for s in range(shards):
+        back_tiles[s] = state.astype(BF16)
+        state = a_rows[s : s + 1, :] * state + b_rows[s : s + 1, :] * got_tiles[s].astype(F32)
+
+    def send_back(peer):
+        remote(
+            back_tiles.at[peer], mem_tiles.at[me], tile_sem.at[2], tile_sem.at[3], seq_at(peer)
+        ).start()
+
+    for y in range(2):
+        for z in range(2):
+            pl.when((my_y != y) | (my_z != z))(functools.partial(send_back, y * SIDE + z))
+    for step in steps:
+        peer = peer_at(step)
+        late = (peer // SIDE >= 2) | (peer % SIDE >= 2)
+        pl.when(late)(functools.partial(send_back, peer))
+    mem_tiles[me] = back_tiles[me]
+
     m_in = m_rows[pl.ds(me, 1), :][:, 0:1]
     begin_full = jnp.concatenate([begin_col] * (tokens // 128), axis=1)
     allowed = (s_full <= t_full) & (s_full >= begin_full)
@@ -320,25 +347,6 @@
     num_ref[...] = jnp.dot(weights.astype(BF16), value, preferred_element_type=F32)
     den_inside = jnp.sum(weights, axis=1, keepdims=True)
 
-    most_tiles = pl.ds(0, shards - 1)
-    remote(
-        got_tiles.at[most_tiles],
-        got_tiles.at[most_tiles],
-        tile_sem.at[0],
-        tile_sem.at[1],
-        seq_at(me),
-    ).wait_recv()
-    state = jnp.zeros((16, 128), F32)
-    for s in range(shards):
-        back_tiles[s] = state.astype(BF16)
-        state = a_rows[s : s + 1, :] * state + b_rows[s : s + 1, :] * got_tiles[s].astype(F32)
-
-    for step in steps:
-        peer = peer_at(step)
-        remote(
-            back_tiles.at[peer], mem_tiles.at[me], tile_sem.at[2], tile_sem.at[3], seq_at(peer)
-        ).start()
-    mem_tiles[me] = back_tiles[me]
 
     some_y = pl.ds(0, rows - 1)
     remote(

time: 46.4 us -> 45.8 us (0.987)
  the two profiles are of different devices: /device:TPU:1 before, /device:TPU:16 now
where the time goes in v3:
time: 45.8 us; the launch traced here: 45.6 us
  Pallas kernels  45 us (98%)
  local copies, waits for them, and re-layouts  0.66 us (1%)
    pallas_call x1, Pallas kernels, on_device(): pl.pallas_call(functools.partial(kernel, shards, chips), out_shape=jax.Sh...  45 us

profile of v3, /device:TPU:16, one launch (start us, length us, event | category | flops | bytes accessed | tf_op | source)
XLA Modules:
  0.0 45.6 jit_solution(744387653470256961)
XLA Ops:
  0.0 45.0 %shard_map.82 = bf16[256,256]{1,0:T(8,128)(2,1)S(1)} custom-call(s32[4]{0:T(128)} %len_hbm.1, bf16[256,256]{1,0:T(8,128)(2,1)} %q_hbm.1, bf16[256,256]{1,0:T(8,128)(2,1)} %k_hbm.1, bf16[256,512]{1,0:T(8,128)(2,1)} %v_hbm.1, f32[2,4,256]{2,1,0:T(4,128)} %taps_hbm.1, f32[1,256]{1,0:T(1,128)} %ig_hbm.1, f32[1,256]{1,0:T(1,128)} %fg_hbm.1, bf16[512,2048]{1,0:T(8,128)(2,1)} %wo_hbm.1), custom_call_target="tpu_custom_call" | custom-call | tf_op jit(solution)/shard_map/pallas_call | solution.py:490
  45.0 0.7 %copy.10 = bf16[256,256]{1,0:T(8,128)(2,1)} copy(bf16[256,256]{1,0:T(8,128)(2,1)S(1)} %shard_map.82) | data formatting | bytes 262144

commit v4 on v3

--- a/solution.py
+++ b/solution.py
@@ -327,14 +327,27 @@
             back_tiles.at[peer], mem_tiles.at[me], tile_sem.at[2], tile_sem.at[3], seq_at(peer)
         ).start()
 
-    for y in range(2):
-        for z in range(2):
-            pl.when((my_y != y) | (my_z != z))(functools.partial(send_back, y * SIDE + z))
+    def to_first(step):
+        peer = ((my_y + step) % rows) * SIDE
+        pl.when((peer != 0) & (peer != me))(functools.partial(send_back, peer))
+
+    def to_other(step):
+        peer = peer_at(step)
+        pl.when(peer % SIDE != 0)(functools.partial(send_back, peer))
+
+    for step in (4, 3, 5, 2, 6, 1, 7, 0):
+        to_first(step)
     for step in steps:
-        peer = peer_at(step)
-        late = (peer // SIDE >= 2) | (peer % SIDE >= 2)
-        pl.when(late)(functools.partial(send_back, peer))
-    mem_tiles[me] = back_tiles[me]
+        to_other(step)
+
+    @pl.when(me == 0)
+    def _():
+        mem_tiles[...] = jnp.zeros(mem_tiles.shape, BF16)
+
+    @pl.when(me != 0)
+    def _():
+        mem_tiles[me] = back_tiles[me]
+
 
     m_in = m_rows[pl.ds(me, 1), :][:, 0:1]
     begin_full = jnp.concatenate([begin_col] * (tokens // 128), axis=1)
@@ -369,13 +382,16 @@
     inverse = 1.0 / floor
 
     loads[6].wait()
-    remote(
-        mem_tiles.at[most_tiles],
-        mem_tiles.at[most_tiles],
-        tile_sem.at[2],
-        tile_sem.at[3],
-        seq_at(me),
-    ).wait_recv()
+    @pl.when(me != 0)
+    def _():
+        remote(
+            mem_tiles.at[most_tiles],
+            mem_tiles.at[most_tiles],
+            tile_sem.at[2],
+            tile_sem.at[3],
+            seq_at(me),
+        ).wait_recv()
+
     parts = []
     for c in range(values // 128):
         block = mem_tiles[c * tile_rows : (c + 1) * tile_rows].reshape(width, 128)
@@ -458,14 +474,20 @@
     remote(
         norm_y.at[some_y], norm_y.at[some_y], norm_sem.at[2], norm_sem.at[3], seq_at(me)
     ).wait_send()
-    for first, tiles in ((0, own_tiles), (2, back_tiles)):
-        remote(
-            tiles.at[most_tiles],
-            tiles.at[most_tiles],
-            tile_sem.at[first],
-            tile_sem.at[first + 1],
-            seq_at(me),
+    remote(
+        own_tiles.at[most_tiles], own_tiles.at[most_tiles], tile_sem.at[0], tile_sem.at[1], seq_at(me)
+    ).wait_send()
+    back_sent = pl.ds(0, shards - 2)
+    remote(
+        back_tiles.at[back_sent], back_tiles.at[back_sent], tile_sem.at[2], tile_sem.at[3], seq_at(me)
+    ).wait_send()
+
+    @pl.when(me == 0)
+    def _():
+        remote(
+            back_tiles.at[0], back_tiles.at[0], tile_sem.at[2], tile_sem.at[3], seq_at(me)
         ).wait_send()
+
     for copy in list(pair_copies.values()) + x_copies:
         copy.wait_send()
 

time: 45.8 us -> 45.4 us (level)
  the two profiles are of different devices: /device:TPU:16 before, /device:TPU:8 now
where the time goes in v4:
time: 45.4 us; the launch traced here: 45.2 us
  Pallas kernels  44.6 us (98%)
  local copies, waits for them, and re-layouts  0.66 us (1%)
    pallas_call x1, Pallas kernels, on_device(): pl.pallas_call(functools.partial(kernel, shards, chips), out_shape=jax.Sh...  44.6 us

profile of v4, /device:TPU:8, one launch (start us, length us, event | category | flops | bytes accessed | tf_op | source)
XLA Modules:
  0.0 45.2 jit_solution(17764262124559441791)
XLA Ops:
  0.0 44.6 %shard_map.82 = bf16[256,256]{1,0:T(8,128)(2,1)S(1)} custom-call(s32[4]{0:T(128)} %len_hbm.1, bf16[256,256]{1,0:T(8,128)(2,1)} %q_hbm.1, bf16[256,256]{1,0:T(8,128)(2,1)} %k_hbm.1, bf16[256,512]{1,0:T(8,128)(2,1)} %v_hbm.1, f32[2,4,256]{2,1,0:T(4,128)} %taps_hbm.1, f32[1,256]{1,0:T(1,128)} %ig_hbm.1, f32[1,256]{1,0:T(1,128)} %fg_hbm.1, bf16[512,2048]{1,0:T(8,128)(2,1)} %wo_hbm.1), custom_call_target="tpu_custom_call" | custom-call | tf_op jit(solution)/shard_map/pallas_call | solution.py:512
  44.6 0.7 %copy.10 = bf16[256,256]{1,0:T(8,128)(2,1)} copy(bf16[256,256]{1,0:T(8,128)(2,1)S(1)} %shard_map.82) | data formatting | bytes 262144

commit v5 on v4

--- a/solution.py
+++ b/solution.py
@@ -425,40 +425,66 @@
         pair_copies[step].wait_recv()
         return ours + pair_recv[step].astype(F32)
 
-    def x_copy(slot, where):
+    quarter = half // 2
+
+    def x_copy(index, slot, count, where):
+        slots = pl.ds(slot, count)
         return remote(
-            x_send.at[slot], x_recv.at[slot], x_ssem.at[slot], x_rsem.at[slot], head_at(where)
-        )
-
-    x_copies = [x_copy(slot, x_next if slot % 2 == 0 else x_prev) for slot in range(6)]
+            x_send.at[slots], x_recv.at[slots], x_ssem.at[index], x_rsem.at[index], head_at(where)
+        )
+
+    x_copies = [
+        x_copy(index, slot, count, where)
+        for index, (slot, count, where) in enumerate(
+            (
+                (0, 1, x_next),
+                (1, 1, x_next),
+                (2, 1, x_prev),
+                (3, 1, x_prev),
+                (4, 2, x_next),
+                (6, 2, x_prev),
+                (8, 1, x_next),
+                (9, 1, x_next),
+                (10, 1, x_prev),
+                (11, 1, x_prev),
+            )
+        )
+    ]
+
+    def rows_of(block, index):
+        return block[index * quarter : (index + 1) * quarter]
+
     pair_start(2)
     pair_start(1)
     pair_start(3)
     pair_start(0)
     opposite = chip_sum(2)
-    x_send[0] = opposite[:half].astype(BF16)
-    x_copies[0].start()
-    x_send[1] = opposite[half:].astype(BF16)
-    x_copies[1].start()
+    for index in (0, 2, 1, 3):
+        x_send[index] = rows_of(opposite, index).astype(BF16)
+        x_copies[index].start()
     after = chip_sum(1)
-    x_send[2] = after[half:].astype(BF16)
-    x_copies[2].start()
+    for index in (2, 3):
+        x_send[2 + index] = rows_of(after, index).astype(BF16)
+    x_copies[4].start()
     before = chip_sum(3)
-    x_send[3] = before[:half].astype(BF16)
-    x_copies[3].start()
-    x_copies[0].wait_recv()
-    x_send[4] = (after[:half] + x_recv[0].astype(F32)).astype(BF16)
-    x_copies[4].start()
-    x_copies[1].wait_recv()
-    x_send[5] = (before[half:] + x_recv[1].astype(F32)).astype(BF16)
+    for index in (0, 1):
+        x_send[6 + index] = rows_of(before, index).astype(BF16)
     x_copies[5].start()
+    for index in (0, 2, 1, 3):
+        x_copies[index].wait_recv()
+        block = after if index < 2 else before
+        x_send[8 + index] = (rows_of(block, index) + x_recv[index].astype(F32)).astype(BF16)
+        x_copies[6 + index].start()
     both = chip_sum(0)
-    x_copies[3].wait_recv()
     x_copies[4].wait_recv()
-    out_ref[:half] = (both[:half] + x_recv[3].astype(F32) + x_recv[4].astype(F32)).astype(BF16)
-    x_copies[2].wait_recv()
     x_copies[5].wait_recv()
-    out_ref[half:] = (both[half:] + x_recv[2].astype(F32) + x_recv[5].astype(F32)).astype(BF16)
+    for index in (0, 2, 1, 3):
+        straight = x_recv[6 + index] if index < 2 else x_recv[2 + index]
+        part = rows_of(both, index) + straight.astype(F32)
+        x_copies[6 + index].wait_recv()
+        out_ref[index * quarter : (index + 1) * quarter] = (
+            part + x_recv[8 + index].astype(F32)
+        ).astype(BF16)
 
     for copy in halos:
         copy.wait_send()
@@ -545,8 +571,8 @@
             pltpu.VMEM((tokens, values), F32),
             pltpu.VMEM((chips, tokens, out_cols), BF16),
             pltpu.VMEM((chips, tokens, out_cols), BF16),
-            pltpu.VMEM((6, tokens // 2, out_cols), BF16),
-            pltpu.VMEM((6, tokens // 2, out_cols), BF16),
+            pltpu.VMEM((12, tokens // 4, out_cols), BF16),
+            pltpu.VMEM((12, tokens // 4, out_cols), BF16),
             dma((8,)),
             dma((4,)),
             dma((4,)),
@@ -554,8 +580,8 @@
             dma((4,)),
             dma((chips,)),
             dma((chips,)),
-            dma((6,)),
-            dma((6,)),
+            dma((10,)),
+            dma((10,)),
             pltpu.SemaphoreType.REGULAR,
         ],
         compiler_params=pltpu.CompilerParams(

time: 45.4 us -> 45 us (level)
  no operation moved by 1% of the time
where the time goes in v5:
time: 45 us; the launch traced here: 44.9 us
  Pallas kernels  44.3 us (98%)
  local copies, waits for them, and re-layouts  0.66 us (1%)
    pallas_call x1, Pallas kernels, on_device(): pl.pallas_call(functools.partial(kernel, shards, chips), out_shape=jax.Sh...  44.3 us

profile of v5, /device:TPU:8, one launch (start us, length us, event | category | flops | bytes accessed | tf_op | source)
XLA Modules:
  0.0 44.9 jit_solution(16378743200374951189)
XLA Ops:
  0.0 44.3 %shard_map.82 = bf16[256,256]{1,0:T(8,128)(2,1)S(1)} custom-call(s32[4]{0:T(128)} %len_hbm.1, bf16[256,256]{1,0:T(8,128)(2,1)} %q_hbm.1, bf16[256,256]{1,0:T(8,128)(2,1)} %k_hbm.1, bf16[256,512]{1,0:T(8,128)(2,1)} %v_hbm.1, f32[2,4,256]{2,1,0:T(4,128)} %taps_hbm.1, f32[1,256]{1,0:T(1,128)} %ig_hbm.1, f32[1,256]{1,0:T(1,128)} %fg_hbm.1, bf16[512,2048]{1,0:T(8,128)(2,1)} %wo_hbm.1), custom_call_target="tpu_custom_call" | custom-call | tf_op jit(solution)/shard_map/pallas_call | solution.py:538
  44.3 0.7 %copy.10 = bf16[256,256]{1,0:T(8,128)(2,1)} copy(bf16[256,256]{1,0:T(8,128)(2,1)S(1)} %shard_map.82) | data formatting | bytes 262144

commit v6 on v5

--- a/solution.py
+++ b/solution.py
@@ -322,9 +322,15 @@
         back_tiles[s] = state.astype(BF16)
         state = a_rows[s : s + 1, :] * state + b_rows[s : s + 1, :] * got_tiles[s].astype(F32)
 
+    my_half = my_y // (rows // 2)
+
     def send_back(peer):
         remote(
-            back_tiles.at[peer], mem_tiles.at[me], tile_sem.at[2], tile_sem.at[3], seq_at(peer)
+            back_tiles.at[peer],
+            mem_tiles.at[me],
+            tile_sem.at[2],
+            tile_sem.at[3 + my_half],
+            seq_at(peer),
         ).start()
 
     def to_first(step):
@@ -346,7 +352,9 @@
 
     @pl.when(me != 0)
     def _():
-        mem_tiles[me] = back_tiles[me]
+        pltpu.make_async_copy(
+            back_tiles.at[me], mem_tiles.at[me], tile_sem.at[3 + my_half]
+        ).start()
 
 
     m_in = m_rows[pl.ds(me, 1), :][:, 0:1]
@@ -382,23 +390,28 @@
     inverse = 1.0 / floor
 
     loads[6].wait()
-    @pl.when(me != 0)
-    def _():
-        remote(
-            mem_tiles.at[most_tiles],
-            mem_tiles.at[most_tiles],
-            tile_sem.at[2],
-            tile_sem.at[3],
-            seq_at(me),
-        ).wait_recv()
-
-    parts = []
-    for c in range(values // 128):
-        block = mem_tiles[c * tile_rows : (c + 1) * tile_rows].reshape(width, 128)
-        from_memory = jnp.dot(query, block, preferred_element_type=F32)
-        at = slice(c * 128, (c + 1) * 128)
-        parts.append(((num_ref[:, at] + reach * from_memory) * inverse).astype(BF16))
-    head_out = jnp.concatenate(parts, axis=1)
+    def head_half(which):
+        tiles = pl.ds(which * shards // 2, shards // 2)
+
+        @pl.when(me != 0)
+        def _():
+            remote(
+                mem_tiles.at[tiles],
+                mem_tiles.at[tiles],
+                tile_sem.at[2],
+                tile_sem.at[3 + which],
+                seq_at(me),
+            ).wait_recv()
+
+        parts = []
+        for c in range(which * values // 256, (which + 1) * values // 256):
+            block = mem_tiles[c * tile_rows : (c + 1) * tile_rows].reshape(width, 128)
+            from_memory = jnp.dot(query, block, preferred_element_type=F32)
+            at = slice(c * 128, (c + 1) * 128)
+            parts.append(((num_ref[:, at] + reach * from_memory) * inverse).astype(BF16))
+        return jnp.concatenate(parts, axis=1)
+
+    head_out = jnp.concatenate([head_half(0), head_half(1)], axis=1)
 
     out_cols = out_ref.shape[1]
     half = tokens // 2
@@ -577,7 +590,7 @@
             dma((4,)),
             dma((4,)),
             dma((4,)),
-            dma((4,)),
+            dma((5,)),
             dma((chips,)),
             dma((chips,)),
             dma((10,)),

time: 45 us -> 45 us (level)
  no operation moved by 1% of the time
where the time goes in v6:
time: 45 us; the launch traced here: 44.9 us
  Pallas kernels  44.2 us (98%)
  local copies, waits for them, and re-layouts  0.66 us (1%)
    pallas_call x1, Pallas kernels, on_device(): pl.pallas_call(functools.partial(kernel, shards, chips), out_shape=jax.Sh...  44.2 us

profile of v6, /device:TPU:8, one launch (start us, length us, event | category | flops | bytes accessed | tf_op | source)
XLA Modules:
  0.0 44.9 jit_solution(7365263759152320267)
XLA Ops:
  0.0 44.2 %shard_map.82 = bf16[256,256]{1,0:T(8,128)(2,1)S(1)} custom-call(s32[4]{0:T(128)} %len_hbm.1, bf16[256,256]{1,0:T(8,128)(2,1)} %q_hbm.1, bf16[256,256]{1,0:T(8,128)(2,1)} %k_hbm.1, bf16[256,512]{1,0:T(8,128)(2,1)} %v_hbm.1, f32[2,4,256]{2,1,0:T(4,128)} %taps_hbm.1, f32[1,256]{1,0:T(1,128)} %ig_hbm.1, f32[1,256]{1,0:T(1,128)} %fg_hbm.1, bf16[512,2048]{1,0:T(8,128)(2,1)} %wo_hbm.1), custom_call_target="tpu_custom_call" | custom-call | tf_op jit(solution)/shard_map/pallas_call | solution.py:551
  44.2 0.7 %copy.10 = bf16[256,256]{1,0:T(8,128)(2,1)} copy(bf16[256,256]{1,0:T(8,128)(2,1)S(1)} %shard_map.82) | data formatting | bytes 262144
